TPU v7x, 32 devices: a whole 2x2x4 slice. The times are simulated.
32 devices in a mesh: grid: 4 (over y, core), tile: 8 (over z, x).
Axes of the slice: x: 2, y: 2, z: 4, core: 2. Of those that a mesh axis runs over, the one named last changes fastest.
Arguments:
- state_field: float32 [4, 128, 4, 4, 4, 4, 128], P('grid', 'tile'), may hold values from -6 to 6
- levels: int32 [4, 6], P('grid'), may hold values from 1 to 4
- sign_bits: int32 [4], P('grid'), may hold values from 0 to 1
Outputs:
- combined_field: float32 [4, 128, 4, 4, 4, 4, 128], P('grid', 'tile')
All inputs are finite; a program needn't handle non-finite values.
Results may differ from a plain program's by a relative error of at most 0.0003.
Values sent between devices are 32-bit elements; how exact they have to be, the bound alone decides.
A program may use at most 64 MiB of HBM per device.

v0:
```python
import functools

import jax
import jax.numpy as jnp
from jax import lax
from jax.experimental import pallas as pl
from jax.experimental.pallas import tpu as pltpu
from jax.sharding import PartitionSpec as P

STEPS = 4
ALPHA = 0.08
BETA = 0.0125


def rate_of(level):
    return jnp.where(
        level >= 4, 1.0, jnp.where(level == 3, 0.5, jnp.where(level == 2, 0.25, 0.125))
    ).astype(jnp.float32)


def kernel(
    grids, tiles, X, B,
    levels_hbm, sign_hbm, x_ref, o_ref,
    levels_ref, sign_ref, u0, halo, pa, ma, pb, mb, val, from_pair, part, from_far, comb, after,
    load_sem, halo_send, halo_recv, pair_send, pair_recv, far_send, far_recv,
    back_send, back_recv, next_send, next_recv,
):
    H = STEPS
    g = lax.axis_index("grid")
    t = lax.axis_index("tile")
    core = g % 2
    pair = g + 1 - 2 * core
    right = (t + 1) % tiles
    left = (t + tiles - 1) % tiles
    far = grids // 2

    def to(grid_at, tile_at):
        return {"grid": grid_at, "tile": tile_at}

    def remote(src, dst, send, recv, where):
        return pltpu.make_async_remote_copy(
            src_ref=src, dst_ref=dst, send_sem=send, recv_sem=recv,
            device_id=where, device_id_type=pl.DeviceIdType.MESH,
        )

    load = pltpu.make_async_copy(x_ref, u0, load_sem.at[0])
    load.start()
    load_levels = pltpu.make_async_copy(levels_hbm, levels_ref, load_sem.at[1])
    load_levels.start()
    load_sign = pltpu.make_async_copy(sign_hbm, sign_ref, load_sem.at[2])
    load_sign.start()

    barrier = pltpu.get_barrier_semaphore()
    others = [to(g, left), to(g, right), to(pair, t)]
    others += [to((g + 2 * k) % grids, t) for k in range(1, far)]
    for other in others:
        pl.semaphore_signal(barrier, inc=1, device_id=other, device_id_type=pl.DeviceIdType.MESH)
    pl.semaphore_wait(barrier, len(others))

    lead = t % 2

    def outward(side, k):
        return remote(
            x_ref.at[k + side * (X - 1 - 2 * k)], halo.at[1 - side, k],
            halo_send.at[side, k], halo_recv.at[1 - side, k],
            to(g, (t + tiles - 1 + 2 * side) % tiles),
        )

    for k in range(H):
        outward(lead, k).start()
    for k in range(H):
        outward(1 - lead, k).start()
    load_levels.wait()
    load_sign.wait()

    rates = [rate_of(levels_ref[0, d]) for d in range(6)]
    total = rates[0] + rates[1] + rates[2] + rates[3] + rates[4] + rates[5]
    centre = 1.0 / (2.0 * ALPHA) - total
    sign = (2 * sign_ref[0] - 1).astype(jnp.float32)

    blocks = 4
    sub = lax.broadcasted_iota(jnp.int32, (B, 8, 128), 1)
    low = sub < 4
    first = sub % 4 == 0
    last = sub % 4 == 3

    def split(u, p_ref, m_ref, layer, rows):
        bent = BETA * u
        p_ref[layer, rows] = u * (ALPHA - bent)
        m_ref[layer, rows] = u * (ALPHA + bent)

    def convert(src, p_ref, m_ref, layer):
        def body(i, carry):
            rows = pl.ds(pl.multiple_of(i * B, B), B)
            split(src[rows], p_ref, m_ref, layer, rows)
            return carry
        lax.fori_loop(0, blocks, body, 0)

    sub = lax.broadcasted_iota(jnp.int32, (2, 8, 128), 1)
    low = sub < 4
    first = sub % 4 == 0
    last = sub % 4 == 3
    fine = blocks * blocks

    def swapped(v):
        return jnp.concatenate([v[1:2], v[0:1]], 0)

    def at_rows(i):
        return pl.ds(i * 2, 2)

    def stencil(p_ref, m_ref, layer, i):
        rows = at_rows(i)
        p = p_ref[layer, rows]
        m = m_ref[layer, rows]
        p5 = pltpu.roll(p, 127, 2)
        m5 = pltpu.roll(m, 1, 2)
        acc = centre * (p + m)
        acc += rates[0] * (p_ref[layer + 1, rows] + m_ref[layer - 1, rows])
        i1, i2 = i // blocks * blocks, i % blocks
        acc += rates[1] * (
            p_ref[layer, at_rows((i + blocks) % fine)]
            + m_ref[layer, at_rows((i + fine - blocks) % fine)]
        )
        acc += rates[2] * (
            p_ref[layer, at_rows(i1 + (i2 + 1) % blocks)]
            + m_ref[layer, at_rows(i1 + (i2 + blocks - 1) % blocks)]
        )
        ph = pltpu.roll(p, 4, 1)
        mh = pltpu.roll(m, 4, 1)
        acc += rates[3] * (jnp.where(low, ph, swapped(ph)) + jnp.where(low, swapped(mh), mh))
        p4 = pltpu.roll(jnp.where(first, ph, p), 7, 1)
        m4 = pltpu.roll(jnp.where(last, mh, m), 1, 1)
        acc += rates[4] * (p4 + m4)
        acc += rates[5] * (p5 + m5)
        return acc, rows

    state = [(pa, ma), (pb, mb)]

    def step(at, lo, count):
        src, dst = state[at % 2], state[(at + 1) % 2]

        def body(i, carry):
            layer = i + (lo + H)
            for n in range(fine):
                acc, rows = stencil(*src, layer, n)
                if at == STEPS - 1:
                    val[layer - H, rows] = sign * acc
                else:
                    split(acc, *dst, layer, rows)
            return carry
        lax.fori_loop(0, count, body, 0)

    chunks = [(at, H) for at in range(H, X - H, H)]
    inner = len(chunks)
    W = H // 2
    for side in (lead, 1 - lead):
        for q in range(2):
            near = H - (q + 1) * W
            chunks.append((near + side * (X - W - 2 * near), W))
    half = B * blocks // 2
    mine = pl.ds(pl.multiple_of(core * half, half), half)
    theirs = pl.ds(pl.multiple_of((1 - core) * half, half), half)

    def layers(j):
        return pl.ds(chunks[j][0], chunks[j][1])

    def pair_copy(j):
        return remote(
            val.at[layers(j), theirs], from_pair.at[layers(j)],
            pair_send.at[j], pair_recv.at[j], to(pair, t),
        )

    def far_copy(j, k):
        return remote(
            part.at[layers(j)], from_far.at[k - 1, layers(j)],
            far_send.at[k - 1, j], far_recv.at[k - 1, j], to((g + 2 * k) % grids, t),
        )

    def back_copy(j):
        own = comb.at[layers(j), mine]
        return remote(own, own, back_send.at[j], back_recv.at[j], to(pair, t))

    def reduce_pair(j):
        pair_copy(j).wait_recv()

        def body(w, carry):
            i = chunks[j][0] + w
            part[i] = val[i, mine] + from_pair[i]
            return carry
        lax.fori_loop(0, chunks[j][1], body, 0)
        for k in range(1, far):
            far_copy(j, k).start()

    def reduce_far(j):
        for k in range(1, far):
            far_copy(j, k).wait_recv()

        def body(w, carry):
            i = chunks[j][0] + w
            summed = part[i]
            for k in range(1, far):
                summed += from_far[k - 1, i]
            comb[i, mine] = summed
            return carry
        lax.fori_loop(0, chunks[j][1], body, 0)
        back_copy(j).start()

    def front(side, lo, hi):
        def mirrored(at):
            return at + side * (X - 1 - 2 * at)

        def wave(k, carry):
            outward(1 - side, k).wait_recv()
            convert(halo.at[side, k], pa, ma, H + mirrored(-1 - k))
            for at in range(STEPS):
                step(at, mirrored(at - k), 1)
            return carry
        lax.fori_loop(lo, hi, wave, 0)

    load.wait()

    def convert_all(i, carry):
        convert(u0.at[i], pa, ma, i + H)
        return carry
    lax.fori_loop(0, X, convert_all, 0)

    for at in range(STEPS):
        step(at, at + 1, 3 * H - 2 - 2 * at)
    pair_copy(0).start()
    for j in range(1, inner):
        for at in range(STEPS):
            step(at, chunks[j][0] + H - 1 - at, H)
            if j == 1 and at == 0:
                reduce_pair(0)
        pair_copy(j).start()
        if j > 1:
            reduce_pair(j - 1)
    front(lead, 0, W)
    pair_copy(inner).start()
    reduce_pair(inner - 1)
    front(lead, W, H)
    pair_copy(inner + 1).start()
    reduce_pair(inner)
    front(1 - lead, 0, W)
    pair_copy(inner + 2).start()
    reduce_pair(inner + 1)
    reduce_far(0)
    front(1 - lead, W, H)
    pair_copy(inner + 3).start()
    reduce_pair(inner + 2)
    for j in range(1, inner):
        reduce_far(j)
    reduce_pair(inner + 3)
    reduce_far(inner)
    reduce_far(inner + 1)
    following = remote(comb.at[0], after, next_send, next_recv, to(g, left))
    back_copy(inner + 1).wait_recv()

    @pl.when(lead == 0)
    def _():
        following.start()

    reduce_far(inner + 2)
    reduce_far(inner + 3)
    back_copy(inner + 3).wait_recv()

    @pl.when(lead == 1)
    def _():
        following.start()

    for j in list(range(inner + 1)) + [inner + 2]:
        back_copy(j).wait_recv()

    level = levels_ref[0, 0]

    def weighted(i, carry):
        layer = i // blocks
        rows = pl.ds(pl.multiple_of((i % blocks) * B, B), B)
        two, four, eight = layer // 2 * 2, layer // 4 * 4, layer // 8 * 8
        anchor = jnp.where(
            level >= 4, layer, jnp.where(level == 3, two, jnp.where(level == 2, four, eight))
        )
        spacing = jnp.where(level >= 4, 1, jnp.where(level == 3, 2, jnp.where(level == 2, 4, 8)))
        weight = (layer - anchor).astype(jnp.float32) * rates[0]
        o_ref[layer, rows] = (1.0 - weight) * comb[anchor, rows] + weight * comb[anchor + spacing, rows]
        return carry

    reach = 8
    lax.fori_loop(0, (X - reach) * blocks, weighted, 0, unroll=4)
    following.wait_recv()
    comb[X] = after[...]
    lax.fori_loop((X - reach) * blocks, X * blocks, weighted, 0, unroll=4)

    for k in range(H):
        outward(0, k).wait_send()
        outward(1, k).wait_send()
    for j in range(inner + 4):
        pair_copy(j).wait_send()
        for k in range(1, far):
            far_copy(j, k).wait_send()
        back_copy(j).wait_send()
    following.wait_send()


def solution(mesh):
    grids, tiles = mesh.shape["grid"], mesh.shape["tile"]

    def on_device(state_field, levels, sign_bits):
        X = state_field.shape[1]
        L = state_field.shape[-1]
        V = state_field.size // (X * 8 * L)
        B = V // state_field.shape[2]
        H = STEPS
        N = X // H + 2
        far = grids // 2 - 1
        f32 = jnp.float32
        field = (V, 8, L)
        halved = (V // 2, 8, L)
        dma = pltpu.SemaphoreType.DMA
        result = pl.pallas_call(
            functools.partial(kernel, grids, tiles, X, B),
            out_shape=jax.ShapeDtypeStruct((X, *field), f32),
            in_specs=[pl.BlockSpec(memory_space=pltpu.HBM)] * 3,
            out_specs=pl.BlockSpec(memory_space=pltpu.VMEM),
            scratch_shapes=[
                pltpu.SMEM(levels.shape, jnp.int32),
                pltpu.SMEM(sign_bits.shape, jnp.int32),
                pltpu.VMEM((X, *field), f32),
                pltpu.VMEM((2, H, *field), f32),
                pltpu.VMEM((X + 2 * H, *field), f32),
                pltpu.VMEM((X + 2 * H, *field), f32),
                pltpu.VMEM((X + 2 * H, *field), f32),
                pltpu.VMEM((X + 2 * H, *field), f32),
                pltpu.VMEM((X, *field), f32),
                pltpu.VMEM((X, *halved), f32),
                pltpu.VMEM((X, *halved), f32),
                pltpu.VMEM((far, X, *halved), f32),
                pltpu.VMEM((X + 1, *field), f32),
                pltpu.VMEM(field, f32),
                dma((3,)),
                dma((2, H)),
                dma((2, H)),
                dma((N,)),
                dma((N,)),
                dma((far, N)),
                dma((far, N)),
                dma((N,)),
                dma((N,)),
                dma,
                dma,
            ],
            compiler_params=pltpu.CompilerParams(
                collective_id=0, has_side_effects=True, vmem_limit_bytes=48 * 1024 * 1024
            ),
        )(levels, sign_bits, state_field.reshape(X, *field))
        return result.reshape(state_field.shape)

    placed = (P("grid", "tile", None, None, None, None, None), P("grid", None), P("grid"))
    return jax.shard_map(
        on_device,
        mesh=mesh,
        in_specs=placed,
        out_specs=P("grid", "tile", None, None, None, None, None),
        check_vma=False,
    )
```

profile of v0, /device:TPU:0, one launch (start us, length us, event | category | flops | bytes accessed | tf_op | source)
XLA Modules:
  0.0 47.4 jit_solution(12576546412440554180)
XLA Ops:
  0.7 0.0 copy-start
  0.7 1.6 %copy-done = f32[1,16,4,4,4,4,128]{6,5,4,3,2,1,0:T(4,128)S(1)} copy-done((f32[1,16,4,4,4,4,128]{6,5,4,3,2,1,0:T(4,128)S(1)}, f32[1,16,4,4,4,4,128]{6,5,4,3,2,1,0:T(4,128)}, u32[]{:S(2)}) %copy-start) | copy-done | bytes 2097176
  2.2 0.0 copy-start.1
  2.2 0.7 %copy-done.1 = s32[1,6]{1,0:T(1,128)S(1)} copy-done((s32[1,6]{1,0:T(1,128)S(1)}, s32[1,6]{1,0:T(1,128)}, u32[]{:S(2)}) %copy-start.1) | copy-done | bytes 48
  2.9 43.2 %shard_map.37 = f32[16,32,8,128]{3,2,1,0:T(8,128)S(1)} custom-call(s32[1,6]{1,0:T(1,128)S(1)} %copy-done.1, s32[1]{0:T(128)S(6)} %copy.5.sign_hbm, f32[16,32,8,128]{3,2,1,0:T(8,128)S(1)} %bitcast.3), custom_call_target="tpu_custom_call" | custom-call | tf_op jit(solution)/shard_map/pallas_call | solution.py:320
  46.1 1.3 %copy.6 = f32[1,16,4,4,4,4,128]{6,5,4,3,2,1,0:T(4,128)} copy(f32[1,16,4,4,4,4,128]{6,5,4,3,2,1,0:T(4,128)S(1)} %bitcast.2) | data formatting | bytes 4194304
Async XLA Ops:
  0.7 1.6 %copy-start = (f32[1,16,4,4,4,4,128]{6,5,4,3,2,1,0:T(4,128)S(1)}, f32[1,16,4,4,4,4,128]{6,5,4,3,2,1,0:T(4,128)}, u32[]{:S(2)}) copy-start(f32[1,16,4,4,4,4,128]{6,5,4,3,2,1,0:T(4,128)} %param.3) | copy-start | bytes 6291460
  2.2 0.7 %copy-start.1 = (s32[1,6]{1,0:T(1,128)S(1)}, s32[1,6]{1,0:T(1,128)}, u32[]{:S(2)}) copy-start(s32[1,6]{1,0:T(1,128)} %levels_hbm.1) | copy-start | bytes 76
where the time goes:
time: 47.6 us; the launch traced here: 47.4 us
  Pallas kernels  43.2 us (91%)
  local copies, waits for them, and re-layouts  3.56 us (7%)
  between operations  0.67 us (1%)
    pallas_call x1, Pallas kernels, on_device(): pl.pallas_call(functools.partial(kernel, grids, tiles, X, B), out_shape=j...  43.2 us
    unnamed x5, local copies, waits for them, and re-layouts  3.56 us

commit v1 on v0

v1 whole, which is shorter than its diff:
```python
import functools

import jax
import jax.numpy as jnp
from jax import lax
from jax.experimental import pallas as pl
from jax.experimental.pallas import tpu as pltpu
from jax.sharding import PartitionSpec as P

STEPS = 4
ALPHA = 0.08
BETA = 0.0125
LOADS = 4


def rate_of(level):
    return jnp.where(
        level >= 4, 1.0, jnp.where(level == 3, 0.5, jnp.where(level == 2, 0.25, 0.125))
    ).astype(jnp.float32)


def kernel(
    grids, tiles, X, B,
    levels_hbm, sign_hbm, x_ref, o_ref,
    levels_ref, sign_ref, raw, pa, ma, pb, mb, val, from_pair, part, from_far, comb,
    small_sem, load_sem, halo_send, halo_recv, pair_send, pair_recv, far_send, far_recv,
    back_send, back_recv, next_send, next_recv,
):
    H = STEPS
    g = lax.axis_index("grid")
    t = lax.axis_index("tile")
    core = g % 2
    pair = g + 1 - 2 * core
    right = (t + 1) % tiles
    left = (t + tiles - 1) % tiles
    far = grids // 2

    def to(grid_at, tile_at):
        return {"grid": grid_at, "tile": tile_at}

    def remote(src, dst, send, recv, where):
        return pltpu.make_async_remote_copy(
            src_ref=src, dst_ref=dst, send_sem=send, recv_sem=recv,
            device_id=where, device_id_type=pl.DeviceIdType.MESH,
        )

    piece = X // LOADS

    def load(i):
        return pltpu.make_async_copy(
            x_ref.at[pl.ds(i * piece, piece)], raw.at[pl.ds(H + i * piece, piece)], load_sem.at[i]
        )

    load_levels = pltpu.make_async_copy(levels_hbm, levels_ref, small_sem.at[0])
    load_sign = pltpu.make_async_copy(sign_hbm, sign_ref, small_sem.at[1])
    load_levels.start()
    load_sign.start()
    for i in range(LOADS):
        load(i).start()

    barrier = pltpu.get_barrier_semaphore()
    others = [to(g, left), to(g, right), to(pair, t)]
    others += [to((g + 2 * k) % grids, t) for k in range(1, far)]
    for other in others:
        pl.semaphore_signal(barrier, inc=1, device_id=other, device_id_type=pl.DeviceIdType.MESH)
    pl.semaphore_wait(barrier, len(others))

    def halo(side, k):
        return remote(
            x_ref.at[(1 - side) * (X - 1 - k) + side * k],
            raw.at[(1 - side) * (H - 1 - k) + side * (X + H + k)],
            halo_send.at[side, k], halo_recv.at[side, k],
            to(g, (t + 1 + side * (tiles - 2)) % tiles),
        )

    for k in range(H):
        halo(0, k).start()
    load_levels.wait()
    load_sign.wait()

    rates = [rate_of(levels_ref[0, d]) for d in range(6)]
    total = rates[0] + rates[1] + rates[2] + rates[3] + rates[4] + rates[5]
    centre = 1.0 / (2.0 * ALPHA) - total
    sign = (2 * sign_ref[0] - 1).astype(jnp.float32)

    blocks = 4
    sub = lax.broadcasted_iota(jnp.int32, (2, 8, 128), 1)
    low = sub < 4
    first = sub % 4 == 0
    last = sub % 4 == 3
    fine = blocks * blocks

    def split(u, p_ref, m_ref, layer, rows):
        bent = BETA * u
        p_ref[layer, rows] = u * (ALPHA - bent)
        m_ref[layer, rows] = u * (ALPHA + bent)

    def convert(layer):
        def body(i, carry):
            rows = pl.ds(pl.multiple_of(i * B, B), B)
            split(raw[layer, rows], pa, ma, layer, rows)
            return carry
        lax.fori_loop(0, blocks, body, 0, unroll=2)

    def swapped(v):
        return jnp.concatenate([v[1:2], v[0:1]], 0)

    def at_rows(i):
        return pl.ds(i * 2, 2)

    def stencil(p_ref, m_ref, layer, i):
        rows = at_rows(i)
        p = p_ref[layer, rows]
        m = m_ref[layer, rows]
        p5 = pltpu.roll(p, 127, 2)
        m5 = pltpu.roll(m, 1, 2)
        acc = centre * (p + m)
        acc += rates[0] * (p_ref[layer + 1, rows] + m_ref[layer - 1, rows])
        i1, i2 = i // blocks * blocks, i % blocks
        acc += rates[1] * (
            p_ref[layer, at_rows((i + blocks) % fine)]
            + m_ref[layer, at_rows((i + fine - blocks) % fine)]
        )
        acc += rates[2] * (
            p_ref[layer, at_rows(i1 + (i2 + 1) % blocks)]
            + m_ref[layer, at_rows(i1 + (i2 + blocks - 1) % blocks)]
        )
        ph = pltpu.roll(p, 4, 1)
        mh = pltpu.roll(m, 4, 1)
        acc += rates[3] * (jnp.where(low, ph, swapped(ph)) + jnp.where(low, swapped(mh), mh))
        p4 = pltpu.roll(jnp.where(first, ph, p), 7, 1)
        m4 = pltpu.roll(jnp.where(last, mh, m), 1, 1)
        acc += rates[4] * (p4 + m4)
        acc += rates[5] * (p5 + m5)
        return acc, rows

    state = [(pa, ma), (pb, mb)]

    def step(at, layer):
        src, dst = state[at % 2], state[(at + 1) % 2]
        for n in range(fine):
            acc, rows = stencil(*src, layer, n)
            if at == STEPS - 1:
                val[layer - H, rows] = sign * acc
            else:
                split(acc, *dst, layer, rows)

    half = B * blocks // 2
    mine = pl.ds(pl.multiple_of(core * half, half), half)
    theirs = pl.ds(pl.multiple_of((1 - core) * half, half), half)

    inner = X - 2 * H
    waves = X + 2 * H

    def place(n):
        past = n // inner
        ending = n // (inner + H)
        return n + (1 - past) * H + (past - ending) * (2 * inner + H - 1 - 2 * n - inner)

    def pair_copy(n):
        i = place(n)
        return remote(
            val.at[i, theirs], from_pair.at[i], pair_send.at[n], pair_recv.at[n], to(pair, t)
        )

    def far_copy(n, k):
        i = place(n)
        return remote(
            part.at[i], from_far.at[k - 1, i],
            far_send.at[k - 1, n], far_recv.at[k - 1, n], to((g + 2 * k) % grids, t),
        )

    def back_copy(n):
        own = comb.at[place(n), mine]
        return remote(own, own, back_send.at[n], back_recv.at[n], to(pair, t))

    def reduce_pair(n):
        pair_copy(n).wait_recv()
        i = place(n)
        part[i] = val[i, mine] + from_pair[i]
        for k in range(1, far):
            far_copy(n, k).start()

    def reduce_far(n):
        for k in range(1, far):
            far_copy(n, k).wait_recv()
        i = place(n)
        summed = part[i]
        for k in range(1, far):
            summed += from_far[k - 1, i]
        comb[i, mine] = summed
        back_copy(n).start()

    ahead = [1, 1, 2, 3, 6, 8, 10, 11]
    ahead = [min(n, X) for n in ahead]

    def done_before(w):
        count = 0
        for j, n in enumerate(ahead):
            more = n - (ahead[j - 1] if j else 0)
            count = count + more * jnp.minimum(jnp.maximum(w - (X + j) + 1, 0), 1)
        return count

    def wave(w, carry):
        ending = w // (X + H)
        leftward = w // X - ending
        at = (1 - leftward) * (w - H * ending) + leftward * (X - 1 - w)
        back = 1 - 2 * leftward

        @pl.when((w < X) & (w % piece == 0))
        def _():
            load(w // piece).wait()

        @pl.when(w >= X)
        def _():
            def finish(n, carry):
                reduce_far(n)
                return carry
            lax.fori_loop(done_before(w - 1), done_before(w), finish, 0)
            halo(ending, (w - X) % H).wait_recv()

        @pl.when(w == X + H - 2)
        def _():
            for k in range(H):
                halo(1, k).start()

        convert(at + H)
        for s in range(STEPS):
            @pl.when(w >= 2 * (s + 1))
            def _(s=s):
                step(s, at - back * (s + 1) + H)

        @pl.when(w >= 2 * H)
        def _():
            pair_copy(w - 2 * H).start()

        @pl.when(w >= 2 * H + 1)
        def _():
            reduce_pair(w - 2 * H - 1)
        return carry

    lax.fori_loop(0, waves, wave, 0)

    following = remote(comb.at[0, mine], comb.at[X, mine], next_send.at[0], next_recv.at[0], to(g, left))
    shared = remote(comb.at[X, mine], comb.at[X, mine], next_send.at[1], next_recv.at[1], to(pair, t))

    level = levels_ref[0, 0]
    reach = 8

    def nodes(base, rows):
        return comb[base, rows], comb[base + reach, rows]

    def rebuilt(base, rows, top):
        v = {0: comb[base, rows], reach: comb[base + reach, rows]}
        depth, gap = 2, reach // 2
        while gap >= 1:
            for i in range(gap, reach, 2 * gap):
                mean = 0.5 * (v[i - gap] + v[i + gap])
                if i < top:
                    v[i] = jnp.where(level >= depth, comb[base + i, rows], mean)
                else:
                    v[i] = mean
            depth, gap = depth + 1, gap // 2
        return v

    def write(base, top):
        def body(i, carry):
            rows = pl.ds(pl.multiple_of(i * 2, 2), 2)
            v = rebuilt(base, rows, top)
            for j in range(reach):
                o_ref[base + j, rows] = v[j]
            return carry
        lax.fori_loop(0, B * blocks // 2, body, 0, unroll=2)

    sums = ahead[-1]
    zero = inner + H - 1
    for n in range(sums, zero + 1):
        reduce_far(n)
    following.start()
    reduce_pair(X - 1)
    for n in range(zero + 1):
        back_copy(n).wait_recv()
    for q in range(X // reach - 1):
        write(q * reach, reach)
    for n in range(zero + 1, X - 1):
        reduce_far(n)
    following.wait_recv()
    shared.start()
    for n in range(zero + 1, X - 1):
        back_copy(n).wait_recv()
    shared.wait_recv()
    write(X - reach, reach - 1)
    reduce_far(X - 1)
    back_copy(X - 1).wait_recv()

    def tail(i, carry):
        rows = pl.ds(pl.multiple_of(i * B, B), B)
        o_ref[X - 1, rows] = jnp.where(level >= 4, comb[X - 1, rows], o_ref[X - 1, rows])
        return carry
    lax.fori_loop(0, blocks, tail, 0, unroll=2)

    for k in range(H):
        halo(0, k).wait_send()
        halo(1, k).wait_send()

    def drain(n, carry):
        pair_copy(n).wait_send()
        for k in range(1, far):
            far_copy(n, k).wait_send()
        back_copy(n).wait_send()
        return carry
    lax.fori_loop(0, X, drain, 0)
    following.wait_send()
    shared.wait_send()


def solution(mesh):
    grids, tiles = mesh.shape["grid"], mesh.shape["tile"]

    def on_device(state_field, levels, sign_bits):
        X = state_field.shape[1]
        L = state_field.shape[-1]
        V = state_field.size // (X * 8 * L)
        B = V // state_field.shape[2]
        H = STEPS
        far = grids // 2 - 1
        f32 = jnp.float32
        field = (V, 8, L)
        halved = (V // 2, 8, L)
        dma = pltpu.SemaphoreType.DMA
        state = pltpu.with_memory_space_constraint(state_field.reshape(X, *field), pltpu.HBM)
        levels = pltpu.with_memory_space_constraint(levels, pltpu.HBM)
        result = pl.pallas_call(
            functools.partial(kernel, grids, tiles, X, B),
            out_shape=jax.ShapeDtypeStruct((X, *field), f32),
            in_specs=[pl.BlockSpec(memory_space=pltpu.HBM)] * 3,
            out_specs=pl.BlockSpec(memory_space=pltpu.VMEM),
            scratch_shapes=[
                pltpu.SMEM(levels.shape, jnp.int32),
                pltpu.SMEM(sign_bits.shape, jnp.int32),
                pltpu.VMEM((X + 2 * H, *field), f32),
                pltpu.VMEM((X + 2 * H, *field), f32),
                pltpu.VMEM((X + 2 * H, *field), f32),
                pltpu.VMEM((X + 2 * H, *field), f32),
                pltpu.VMEM((X + 2 * H, *field), f32),
                pltpu.VMEM((X, *field), f32),
                pltpu.VMEM((X, *halved), f32),
                pltpu.VMEM((X, *halved), f32),
                pltpu.VMEM((far, X, *halved), f32),
                pltpu.VMEM((X + 1, *field), f32),
                dma((2,)),
                dma((LOADS,)),
                dma((2, H)),
                dma((2, H)),
                dma((X,)),
                dma((X,)),
                dma((far, X)),
                dma((far, X)),
                dma((X,)),
                dma((X,)),
                dma((2,)),
                dma((2,)),
            ],
            compiler_params=pltpu.CompilerParams(
                collective_id=0, has_side_effects=True, vmem_limit_bytes=48 * 1024 * 1024
            ),
        )(levels, sign_bits, state)
        return result.reshape(state_field.shape)

    placed = (P("grid", "tile", None, None, None, None, None), P("grid", None), P("grid"))
    return jax.shard_map(
        on_device,
        mesh=mesh,
        in_specs=placed,
        out_specs=P("grid", "tile", None, None, None, None, None),
        check_vma=False,
    )
```

time: 47.6 us -> 44.9 us (0.943)
  local copies, waits for them, and re-layouts: 3.56 us -> 1.32 us
    unnamed x5 -> x1, local copies, waits for them, and re-layouts: 3.56 us -> 1.32 us
where the time goes in v1:
time: 44.9 us; the launch traced here: 44.7 us
  Pallas kernels  42.8 us (95%)
  local copies, waits for them, and re-layouts  1.32 us (3%)
  between operations  0.66 us (1%)
    pallas_call x1, Pallas kernels, on_device(): pl.pallas_call(functools.partial(kernel, grids, tiles, X, B), out_shape=j...  42.8 us
    unnamed x1, local copies, waits for them, and re-layouts  1.32 us

profile of v1, /device:TPU:0, one launch (start us, length us, event | category | flops | bytes accessed | tf_op | source)
XLA Modules:
  0.0 44.7 jit_solution(11432015447451714888)
XLA Ops:
  0.7 42.8 %shard_map.37 = f32[16,32,8,128]{3,2,1,0:T(8,128)S(1)} custom-call(s32[1,6]{1,0:T(1,128)} %levels_hbm.1, s32[1]{0:T(128)S(6)} %copy.5.sign_hbm, f32[16,32,8,128]{3,2,1,0:T(8,128)} %bitcast.3), custom_call_target="tpu_custom_call" | custom-call | tf_op jit(solution)/shard_map/pallas_call | solution.py:333
  43.4 1.3 %copy.6 = f32[1,16,4,4,4,4,128]{6,5,4,3,2,1,0:T(4,128)} copy(f32[1,16,4,4,4,4,128]{6,5,4,3,2,1,0:T(4,128)S(1)} %bitcast.2) | data formatting | bytes 4194304

commit v2 on v1

v2 whole, which is shorter than its diff:
```python
import functools

import jax
import jax.numpy as jnp
from jax import lax
from jax.experimental import pallas as pl
from jax.experimental.pallas import tpu as pltpu
from jax.sharding import PartitionSpec as P

STEPS = 4
ALPHA = 0.08
BETA = 0.0125
KAPPA = BETA / ALPHA
LOADS = 4


def rate_of(level):
    return jnp.where(
        level >= 4, 1.0, jnp.where(level == 3, 0.5, jnp.where(level == 2, 0.25, 0.125))
    ).astype(jnp.float32)


def kernel(
    grids, tiles, X, B,
    levels_hbm, sign_hbm, x_ref, o_ref,
    levels_ref, sign_ref, raw, pa, ma, pb, mb, rest, val, from_pair, part, from_far, comb,
    small_sem, load_sem, halo_send, halo_recv, pair_send, pair_recv, far_send, far_recv,
    back_send, back_recv, next_send, next_recv, credit,
):
    H = STEPS
    g = lax.axis_index("grid")
    t = lax.axis_index("tile")
    core = g % 2
    pair = g + 1 - 2 * core
    right = (t + 1) % tiles
    left = (t + tiles - 1) % tiles
    far = grids // 2

    def to(grid_at, tile_at):
        return {"grid": grid_at, "tile": tile_at}

    def remote(src, dst, send, recv, where):
        return pltpu.make_async_remote_copy(
            src_ref=src, dst_ref=dst, send_sem=send, recv_sem=recv,
            device_id=where, device_id_type=pl.DeviceIdType.MESH,
        )

    piece = X // LOADS

    def load(i):
        return pltpu.make_async_copy(
            x_ref.at[pl.ds(i * piece, piece)], raw.at[pl.ds(H + i * piece, piece)], load_sem.at[i]
        )

    load_levels = pltpu.make_async_copy(levels_hbm, levels_ref, small_sem.at[0])
    load_sign = pltpu.make_async_copy(sign_hbm, sign_ref, small_sem.at[1])
    load(0).start()
    load_levels.start()
    load_sign.start()
    barrier = pltpu.get_barrier_semaphore()

    def greet(other):
        pl.semaphore_signal(barrier, inc=1, device_id=other, device_id_type=pl.DeviceIdType.MESH)

    others = [to(g, left), to(pair, t)]
    others += [to((g + 2 * k) % grids, t) for k in range(1, far)]
    for other in others:
        greet(other)

    @pl.when(t < tiles - 1)
    def _():
        greet(to(g, right))

    def give_credit():
        pl.semaphore_signal(
            credit, inc=1, device_id=to(g, right), device_id_type=pl.DeviceIdType.MESH
        )

    for i in range(1, LOADS):
        load(i).start()

    def halo(side, k):
        return remote(
            x_ref.at[(1 - side) * (X - 1 - k) + side * k],
            raw.at[(1 - side) * (H - 1 - k) + side * (X + H + k)],
            halo_send.at[side], halo_recv.at[side, k],
            to(g, (t + 1 + side * (tiles - 2)) % tiles),
        )

    blocks = 4
    sub = lax.broadcasted_iota(jnp.int32, (2, 8, 128), 1)
    low = sub < 4
    first = sub % 4 == 0
    last = sub % 4 == 3
    fine = blocks * blocks

    def split(v, p_ref, m_ref, layer, rows):
        square = v * v
        p_ref[layer, rows] = v - square
        m_ref[layer, rows] = v + square

    def convert(layer):
        for i in range(blocks):
            rows = pl.ds(i * B, B)
            split(KAPPA * raw[layer, rows], pa, ma, layer, rows)

    def convert_from(lo, hi):
        def body(i, carry):
            convert(i + H)
            return carry
        lax.fori_loop(lo, hi, body, 0)

    load(0).wait()
    convert_from(0, piece)
    pl.semaphore_wait(barrier, len(others) + jnp.minimum(t, 1))

    @pl.when(t == tiles - 1)
    def _():
        give_credit()

    for k in range(H):
        halo(0, k).start()

    odd = t % 2

    @pl.when(odd == 1)
    def _():
        for k in range(H):
            halo(1, k).start()

    for lo in range(piece, 2 * H + 1, piece):
        load(lo // piece).wait()
        convert_from(lo, min(lo + piece, 2 * H + 1))
    load_levels.wait()
    load_sign.wait()

    rates = [ALPHA * rate_of(levels_ref[0, d]) for d in range(6)]
    total = rates[0] + rates[1] + rates[2] + rates[3] + rates[4] + rates[5]
    centre = 0.5 - total
    sign = (2 * sign_ref[0] - 1).astype(jnp.float32) * (1.0 / KAPPA)

    def swapped(v):
        return jnp.concatenate([v[1:2], v[0:1]], 0)

    def at_rows(i):
        return pl.ds(i * 2, 2)

    def stencil(p_ref, m_ref, layer, i, upper):
        rows = at_rows(i)
        p = p_ref[layer, rows]
        m = m_ref[layer, rows]
        p5 = pltpu.roll(p, 127, 2)
        m5 = pltpu.roll(m, 1, 2)
        acc = centre * (p + m)
        if upper:
            acc += rates[0] * (p_ref[layer + 1, rows] + m_ref[layer - 1, rows])
        else:
            acc += rates[0] * m_ref[layer - 1, rows]
        i1, i2 = i // blocks * blocks, i % blocks
        acc += rates[1] * (
            p_ref[layer, at_rows((i + blocks) % fine)]
            + m_ref[layer, at_rows((i + fine - blocks) % fine)]
        )
        acc += rates[2] * (
            p_ref[layer, at_rows(i1 + (i2 + 1) % blocks)]
            + m_ref[layer, at_rows(i1 + (i2 + blocks - 1) % blocks)]
        )
        ph = pltpu.roll(p, 4, 1)
        mh = pltpu.roll(m, 4, 1)
        acc += rates[3] * (jnp.where(low, ph, swapped(ph)) + jnp.where(low, swapped(mh), mh))
        p4 = pltpu.roll(jnp.where(first, ph, p), 7, 1)
        m4 = pltpu.roll(jnp.where(last, mh, m), 1, 1)
        acc += rates[4] * (p4 + m4)
        acc += rates[5] * (p5 + m5)
        return acc, rows

    state = [(pa, ma), (pb, mb)]

    def step(at, layer):
        src, dst = state[at % 2], state[(at + 1) % 2]
        for n in range(fine):
            acc, rows = stencil(*src, layer, n, True)
            if at == STEPS - 1:
                val[layer - H, rows] = sign * acc
            else:
                split(acc, *dst, layer, rows)

    def partly(at, layer):
        for n in range(fine):
            acc, rows = stencil(*state[at % 2], layer, n, False)
            rest[at, rows] = acc

    half = B * blocks // 2
    mine = pl.ds(pl.multiple_of(core * half, half), half)
    theirs = pl.ds(pl.multiple_of((1 - core) * half, half), half)

    inner = X - 2 * H

    def place(n):
        past = n // inner
        ending = n // (inner + H)
        return n + (1 - past) * H + (past - ending) * (2 * inner + H - 1 - 2 * n - inner)

    def pair_copy(n):
        i = place(n)
        return remote(val.at[i, theirs], from_pair.at[i], pair_send.at[0], pair_recv.at[n], to(pair, t))

    def far_copy(n, k):
        i = place(n)
        return remote(
            part.at[i], from_far.at[k - 1, i],
            far_send.at[k - 1], far_recv.at[k - 1, n], to((g + 2 * k) % grids, t),
        )

    def back_copy(n):
        own = comb.at[place(n), mine]
        return remote(own, own, back_send.at[0], back_recv.at[n], to(pair, t))

    def reduce_pair(n):
        pair_copy(n).wait_recv()
        i = place(n)
        part[i] = val[i, mine] + from_pair[i]
        for k in range(1, far):
            far_copy(n, k).start()

    def reduce_far(n):
        for k in range(1, far):
            far_copy(n, k).wait_recv()
        i = place(n)
        summed = part[i]
        for k in range(1, far):
            summed += from_far[k - 1, i]
        comb[i, mine] = summed
        back_copy(n).start()

    ahead = [min(n, X) for n in (2, 2, 3, 5, 7, 9, 10)]

    def done_before(j):
        count = 0
        for i, n in enumerate(ahead):
            more = n - (ahead[i - 1] if i else 0)
            count = count + more * jnp.minimum(jnp.maximum(j - i + 1, 0), 1)
        return count

    def finish_far(lo, hi):
        def body(n, carry):
            reduce_far(n)
            return carry
        lax.fori_loop(lo, hi, body, 0)

    for s in range(STEPS):
        def body(i, carry, s=s):
            step(s, i + H)
            return carry
        lax.fori_loop(s + 1, 2 * H - s, body, 0)
    pair_copy(0).start()

    def wave(n, carry):
        ending = n // (inner + H)
        leftward = n // inner - ending
        w = n + 2 * H
        at = (1 - leftward) * (w - H * ending) + leftward * (X - 1 - w)
        back = 1 - 2 * leftward

        @pl.when((n < inner) & (w % piece == 0))
        def _():
            load(w // piece).wait()

        @pl.when(n >= inner + H)
        def _():
            reduce_pair(n - 1)

        @pl.when(n >= inner)
        def _():
            j = n - inner
            more = jnp.maximum(1 - t, 0) * ahead[3]
            finish_far(
                jnp.maximum(done_before(j - 1), more * jnp.minimum(j // 3, 1)),
                jnp.maximum(done_before(j), more * jnp.minimum(j // 2, 1)),
            )

        @pl.when((odd == 0) & (n == inner + 2))
        def _():
            pl.semaphore_wait(credit, 1)
            for k in range(H):
                halo(1, k).start()

        @pl.when((n >= inner) & ((odd == 0) | (t == tiles - 1) | (n != inner + 2)))
        def _():
            halo(ending, (n - inner) % H).wait_recv()

        @pl.when((odd == 1) & (t < tiles - 1) & (n == inner + 1))
        def _():
            halo(ending, 2).wait_recv()
            give_credit()

        convert(at + H)
        for s in range(STEPS):
            step(s, at - back * (s + 1) + H)
        pair_copy(n).start()

        @pl.when(n < inner + H)
        def _():
            reduce_pair(n - 1)
        return carry

    lax.fori_loop(1, X - 1, wave, 0)

    end = X + H - 1
    for s in range(STEPS):
        partly(s, end - 1 - s + H)
    reduce_pair(X - 2)
    zero = inner + H - 1
    finish_far(ahead[-1], zero + 1)
    following = remote(comb.at[0, mine], comb.at[X, mine], next_send.at[0], next_recv.at[0], to(g, left))
    following.start()
    halo(1, H - 1).wait_recv()
    for i in range(blocks):
        rows = pl.ds(i * B, B)
        v = KAPPA * raw[end + H, rows]
        for s in range(STEPS):
            acc = rest[s, rows] + rates[0] * (v - v * v)
            if s == STEPS - 1:
                val[X - 1, rows] = sign * acc
            v = acc
    pair_copy(X - 1).start()

    shared = remote(comb.at[X, mine], comb.at[X, mine], next_send.at[1], next_recv.at[1], to(pair, t))

    level = levels_ref[0, 0]
    reach = 8

    def rebuilt(base, rows, top):
        v = {0: comb[base, rows], reach: comb[base + reach, rows]}
        depth, gap = 2, reach // 2
        while gap >= 1:
            for i in range(gap, reach, 2 * gap):
                mean = 0.5 * (v[i - gap] + v[i + gap])
                v[i] = jnp.where(level >= depth, comb[base + i, rows], mean) if i < top else mean
            depth, gap = depth + 1, gap // 2
        return v

    def write(base, top):
        def body(i, carry):
            rows = pl.ds(pl.multiple_of(i * 2, 2), 2)
            v = rebuilt(base, rows, top)
            for j in range(reach):
                o_ref[base + j, rows] = v[j]
            return carry
        lax.fori_loop(0, B * blocks // 2, body, 0, unroll=2)

    for n in range(zero + 1):
        back_copy(n).wait_recv()
    for q in range(X // reach - 1):
        write(q * reach, reach)
    reduce_pair(X - 1)
    for side in range(2):
        whole = raw.at[pl.ds(0, H)]
        remote(whole, whole, halo_send.at[side], halo_recv.at[side, 0], to(g, left)).wait_send()
    finish_far(zero + 1, X - 1)
    following.wait_recv()
    shared.start()
    reduce_far(X - 1)
    for n in range(zero + 1, X - 1):
        back_copy(n).wait_recv()
    shared.wait_recv()
    write(X - reach, reach - 1)
    following.wait_send()
    remote(part, part, pair_send.at[0], pair_recv.at[0], to(pair, t)).wait_send()
    shared.wait_send()
    back_copy(X - 1).wait_recv()
    for i in range(blocks):
        rows = pl.ds(i * B, B)
        o_ref[X - 1, rows] = jnp.where(level >= 4, comb[X - 1, rows], o_ref[X - 1, rows])
    for k in range(1, far):
        remote(part, part, far_send.at[k - 1], far_recv.at[k - 1, 0], to(pair, t)).wait_send()
    remote(part, part, back_send.at[0], back_recv.at[0], to(pair, t)).wait_send()


def solution(mesh):
    grids, tiles = mesh.shape["grid"], mesh.shape["tile"]

    def on_device(state_field, levels, sign_bits):
        X = state_field.shape[1]
        L = state_field.shape[-1]
        V = state_field.size // (X * 8 * L)
        B = V // state_field.shape[2]
        H = STEPS
        far = grids // 2 - 1
        f32 = jnp.float32
        field = (V, 8, L)
        halved = (V // 2, 8, L)
        dma = pltpu.SemaphoreType.DMA
        state = pltpu.with_memory_space_constraint(state_field.reshape(X, *field), pltpu.HBM)
        levels = pltpu.with_memory_space_constraint(levels, pltpu.HBM)
        result = pl.pallas_call(
            functools.partial(kernel, grids, tiles, X, B),
            out_shape=jax.ShapeDtypeStruct((X, *field), f32),
            in_specs=[pl.BlockSpec(memory_space=pltpu.HBM)] * 3,
            out_specs=pl.BlockSpec(memory_space=pltpu.VMEM),
            scratch_shapes=[
                pltpu.SMEM(levels.shape, jnp.int32),
                pltpu.SMEM(sign_bits.shape, jnp.int32),
                pltpu.VMEM((X + 2 * H, *field), f32),
                pltpu.VMEM((X + 2 * H, *field), f32),
                pltpu.VMEM((X + 2 * H, *field), f32),
                pltpu.VMEM((X + 2 * H, *field), f32),
                pltpu.VMEM((X + 2 * H, *field), f32),
                pltpu.VMEM((H, *field), f32),
                pltpu.VMEM((X, *field), f32),
                pltpu.VMEM((X, *halved), f32),
                pltpu.VMEM((X, *halved), f32),
                pltpu.VMEM((far, X, *halved), f32),
                pltpu.VMEM((X + 1, *field), f32),
                dma((2,)),
                dma((LOADS,)),
                dma((2,)),
                dma((2, H)),
                dma((1,)),
                dma((X,)),
                dma((far,)),
                dma((far, X)),
                dma((1,)),
                dma((X,)),
                dma((2,)),
                dma((2,)),
                pltpu.SemaphoreType.REGULAR,
            ],
            compiler_params=pltpu.CompilerParams(
                collective_id=0, has_side_effects=True, vmem_limit_bytes=48 * 1024 * 1024
            ),
        )(levels, sign_bits, state)
        return result.reshape(state_field.shape)

    placed = (P("grid", "tile", None, None, None, None, None), P("grid", None), P("grid"))
    return jax.shard_map(
        on_device,
        mesh=mesh,
        in_specs=placed,
        out_specs=P("grid", "tile", None, None, None, None, None),
        check_vma=False,
    )
```

time: 44.9 us -> 36.6 us (0.82)
  Pallas kernels: 42.8 us -> 34.5 us
    pallas_call x1, Pallas kernels: 42.8 us -> 34.5 us  [on_device(): pl.pallas_call(functools.partial(kernel, grids, tiles, X, B), out_shape=j...]
where the time goes in v2:
time: 36.6 us; the launch traced here: 36.5 us
  Pallas kernels  34.5 us (94%)
  local copies, waits for them, and re-layouts  1.32 us (4%)
  between operations  0.66 us (2%)
    pallas_call x1, Pallas kernels, on_device(): pl.pallas_call(functools.partial(kernel, grids, tiles, X, B), out_shape=j...  34.5 us
    unnamed x1, local copies, waits for them, and re-layouts  1.32 us

profile of v2, /device:TPU:0, one launch (start us, length us, event | category | flops | bytes accessed | tf_op | source)
XLA Modules:
  0.0 36.5 jit_solution(3636540555329537844)
XLA Ops:
  0.7 34.5 %shard_map.37 = f32[16,32,8,128]{3,2,1,0:T(8,128)S(1)} custom-call(s32[1,6]{1,0:T(1,128)} %levels_hbm.1, s32[1]{0:T(128)S(6)} %copy.5.sign_hbm, f32[16,32,8,128]{3,2,1,0:T(8,128)} %bitcast.3), custom_call_target="tpu_custom_call" | custom-call | tf_op jit(solution)/shard_map/pallas_call | solution.py:396
  35.2 1.3 %copy.6 = f32[1,16,4,4,4,4,128]{6,5,4,3,2,1,0:T(4,128)} copy(f32[1,16,4,4,4,4,128]{6,5,4,3,2,1,0:T(4,128)S(1)} %bitcast.2) | data formatting | bytes 4194304

commit v3 on v2

--- a/solution.py
+++ b/solution.py
@@ -25,7 +25,7 @@
     levels_hbm, sign_hbm, x_ref, o_ref,
     levels_ref, sign_ref, raw, pa, ma, pb, mb, rest, val, from_pair, part, from_far, comb,
     small_sem, load_sem, halo_send, halo_recv, pair_send, pair_recv, far_send, far_recv,
-    back_send, back_recv, next_send, next_recv, credit,
+    back_send, back_recv, next_send, next_recv, credit, met,
 ):
     H = STEPS
     g = lax.axis_index("grid")
@@ -83,11 +83,42 @@
         return remote(
             x_ref.at[(1 - side) * (X - 1 - k) + side * k],
             raw.at[(1 - side) * (H - 1 - k) + side * (X + H + k)],
-            halo_send.at[side], halo_recv.at[side, k],
+            halo_send.at[side], halo_recv.at[side * H + k],
             to(g, (t + 1 + side * (tiles - 2)) % tiles),
         )
 
     blocks = 4
+
+    def last_halo(q):
+        rows = pl.ds(q * B, B)
+        return remote(
+            x_ref.at[H - 1, rows], raw.at[X + 2 * H - 1, rows],
+            halo_send.at[1], halo_recv.at[2 * H - 1 + q], to(g, left),
+        )
+
+    part_at = B
+
+    def third_halo(q):
+        rows = pl.ds(q * part_at, part_at - q * (2 * part_at - blocks * B))
+        return remote(
+            x_ref.at[X - 3, rows], raw.at[H - 3, rows],
+            halo_send.at[0], halo_recv.at[2 + q * (2 * H + 1)], to(g, right),
+        )
+
+    def start_left():
+        for k in range(2):
+            halo(0, k).start()
+        for q in range(2):
+            third_halo(q).start()
+        for k in range(3, H):
+            halo(0, k).start()
+
+    def start_right():
+        for k in range(H - 1):
+            halo(1, k).start()
+        for q in range(blocks):
+            last_halo(q).start()
+
     sub = lax.broadcasted_iota(jnp.int32, (2, 8, 128), 1)
     low = sub < 4
     first = sub % 4 == 0
@@ -118,15 +149,13 @@
     def _():
         give_credit()
 
-    for k in range(H):
-        halo(0, k).start()
+    start_left()
 
     odd = t % 2
 
     @pl.when(odd == 1)
     def _():
-        for k in range(H):
-            halo(1, k).start()
+        start_right()
 
     for lo in range(piece, 2 * H + 1, piece):
         load(lo // piece).wait()
@@ -197,13 +226,15 @@
     inner = X - 2 * H
 
     def place(n):
-        past = n // inner
-        ending = n // (inner + H)
-        return n + (1 - past) * H + (past - ending) * (2 * inner + H - 1 - 2 * n - inner)
+        past = jnp.minimum(n // inner, 1)
+        done = jnp.minimum(n // (X - H), 1)
+        return n + (1 - past) * H + (past - done) * (X - H - 1 - 2 * n)
 
     def pair_copy(n):
         i = place(n)
-        return remote(val.at[i, theirs], from_pair.at[i], pair_send.at[0], pair_recv.at[n], to(pair, t))
+        return remote(
+            val.at[i, theirs], from_pair.at[i], pair_send.at[0], pair_recv.at[n % 4], to(pair, t)
+        )
 
     def far_copy(n, k):
         i = place(n)
@@ -214,7 +245,12 @@
 
     def back_copy(n):
         own = comb.at[place(n), mine]
-        return remote(own, own, back_send.at[0], back_recv.at[n], to(pair, t))
+        group = jnp.minimum(n // (X - H), 1)
+        return remote(own, own, back_send.at[0], back_recv.at[group], to(pair, t))
+
+    def backs_done(group, count):
+        some = part.at[pl.ds(0, count)]
+        remote(some, some, back_send.at[0], back_recv.at[group], to(pair, t)).wait_recv()
 
     def reduce_pair(n):
         pair_copy(n).wait_recv()
@@ -233,20 +269,51 @@
         comb[i, mine] = summed
         back_copy(n).start()
 
-    ahead = [min(n, X) for n in (2, 2, 3, 5, 7, 9, 10)]
+    small = B // 2
+
+    def own_rows(q):
+        return pl.ds(pl.multiple_of(q * B + core * small, small), small)
+
+    def other_rows(q):
+        return pl.ds(pl.multiple_of(q * B + (1 - core) * small, small), small)
+
+    def kept(q):
+        return pl.ds(q * small, small)
+
+    def last_pair(q):
+        return remote(
+            val.at[X - 1, other_rows(q)], from_pair.at[X - 1, kept(q)],
+            pair_send.at[0], pair_recv.at[4 + q], to(pair, t),
+        )
+
+    def last_far(q, k):
+        return remote(
+            part.at[X - 1, kept(q)], from_far.at[k - 1, X - 1, kept(q)],
+            far_send.at[k - 1], far_recv.at[k - 1, X - 1 + q], to((g + 2 * k) % grids, t),
+        )
+
+    def last_back(q):
+        own = comb.at[X - 1, own_rows(q)]
+        return remote(own, own, back_send.at[0], back_recv.at[2], to(pair, t))
+
+    ahead = [2, 2, 3, 5, 7, 9, 10]
+    held = 5
 
     def done_before(j):
         count = 0
         for i, n in enumerate(ahead):
             more = n - (ahead[i - 1] if i else 0)
             count = count + more * jnp.minimum(jnp.maximum(j - i + 1, 0), 1)
-        return count
+        return jnp.maximum(count, jnp.maximum(1 - t, 0) * held * jnp.minimum(jnp.maximum(j - 1, 0), 1))
 
     def finish_far(lo, hi):
         def body(n, carry):
             reduce_far(n)
             return carry
         lax.fori_loop(lo, hi, body, 0)
+
+    following = remote(comb.at[0, mine], comb.at[X, mine], next_send.at[0], next_recv.at[0], to(g, left))
+    shared = remote(comb.at[X, mine], comb.at[X, mine], next_send.at[1], next_recv.at[1], to(pair, t))
 
     for s in range(STEPS):
         def body(i, carry, s=s):
@@ -256,42 +323,45 @@
     pair_copy(0).start()
 
     def wave(n, carry):
-        ending = n // (inner + H)
-        leftward = n // inner - ending
-        w = n + 2 * H
-        at = (1 - leftward) * (w - H * ending) + leftward * (X - 1 - w)
+        leftward = n // inner
         back = 1 - 2 * leftward
-
-        @pl.when((n < inner) & (w % piece == 0))
-        def _():
-            load(w // piece).wait()
-
-        @pl.when(n >= inner + H)
-        def _():
-            reduce_pair(n - 1)
-
-        @pl.when(n >= inner)
-        def _():
-            j = n - inner
-            more = jnp.maximum(1 - t, 0) * ahead[3]
-            finish_far(
-                jnp.maximum(done_before(j - 1), more * jnp.minimum(j // 3, 1)),
-                jnp.maximum(done_before(j), more * jnp.minimum(j // 2, 1)),
+        at = (1 - leftward) * (n + 2 * H) + leftward * (inner - 1 - n)
+        j = n - inner
+
+        @pl.when((leftward == 0) & (at % piece == 0))
+        def _():
+            load(at // piece).wait()
+
+        @pl.when(leftward == 1)
+        def _():
+            finish_far(done_before(j - 1), done_before(j))
+
+        @pl.when((t == 0) & (j == 2))
+        def _():
+            pl.semaphore_wait(credit, 1)
+            start_right()
+
+        @pl.when((leftward == 1) & (j != 2))
+        def _():
+            halo(0, j).wait_recv()
+
+        paced = (odd == 1) & (t < tiles - 1)
+
+        @pl.when((j == 2) & ((odd == 0) | (t == tiles - 1)))
+        def _():
+            third_halo(0).wait_recv()
+
+        @pl.when(j == 2)
+        def _():
+            third_halo(1).wait_recv()
+
+        @pl.when(paced & (j == 0))
+        def _():
+            third_halo(0).wait_recv()
+            pl.semaphore_signal(
+                met, inc=1, device_id=to(pair, t), device_id_type=pl.DeviceIdType.MESH
             )
-
-        @pl.when((odd == 0) & (n == inner + 2))
-        def _():
-            pl.semaphore_wait(credit, 1)
-            for k in range(H):
-                halo(1, k).start()
-
-        @pl.when((n >= inner) & ((odd == 0) | (t == tiles - 1) | (n != inner + 2)))
-        def _():
-            halo(ending, (n - inner) % H).wait_recv()
-
-        @pl.when((odd == 1) & (t < tiles - 1) & (n == inner + 1))
-        def _():
-            halo(ending, 2).wait_recv()
+            pl.semaphore_wait(met, 1)
             give_credit()
 
         convert(at + H)
@@ -299,33 +369,52 @@
             step(s, at - back * (s + 1) + H)
         pair_copy(n).start()
 
-        @pl.when(n < inner + H)
-        def _():
-            reduce_pair(n - 1)
+        @pl.when((odd == 0) & (t > 0) & (j == 1))
+        def _():
+            pl.semaphore_wait(credit, 1)
+            start_right()
+
+        reduce_pair(n - 1)
         return carry
 
-    lax.fori_loop(1, X - 1, wave, 0)
-
-    end = X + H - 1
-    for s in range(STEPS):
-        partly(s, end - 1 - s + H)
-    reduce_pair(X - 2)
-    zero = inner + H - 1
-    finish_far(ahead[-1], zero + 1)
-    following = remote(comb.at[0, mine], comb.at[X, mine], next_send.at[0], next_recv.at[0], to(g, left))
+    lax.fori_loop(1, X - H, wave, 0)
+
+    def prepare(n):
+        for s in range(STEPS):
+            partly(s, n + 2 * H - 1 - s)
+        reduce_pair(n - 1)
+
+    def complete(n, q, keep):
+        rows = pl.ds(q * B, B)
+        v = KAPPA * raw[n + 2 * H, rows]
+        for s in range(STEPS):
+            square = v * v
+            p = v - square
+            if keep:
+                p_ref, m_ref = state[s % 2]
+                p_ref[n + 2 * H - s, rows] = p
+                m_ref[n + 2 * H - s, rows] = v + square
+            v = rest[s, rows] + rates[0] * p
+        val[n, rows] = sign * v
+
+    def ending(n, carry):
+        j = n - inner
+        prepare(n)
+        finish_far(done_before(j - 1), done_before(j))
+        halo(1, n - (X - H)).wait_recv()
+        for q in range(blocks):
+            complete(n, q, True)
+        pair_copy(n).start()
+        return carry
+
+    lax.fori_loop(X - H, X - 1, ending, 0)
+    finish_far(ahead[-1], X - H)
     following.start()
-    halo(1, H - 1).wait_recv()
-    for i in range(blocks):
-        rows = pl.ds(i * B, B)
-        v = KAPPA * raw[end + H, rows]
-        for s in range(STEPS):
-            acc = rest[s, rows] + rates[0] * (v - v * v)
-            if s == STEPS - 1:
-                val[X - 1, rows] = sign * acc
-            v = acc
-    pair_copy(X - 1).start()
-
-    shared = remote(comb.at[X, mine], comb.at[X, mine], next_send.at[1], next_recv.at[1], to(pair, t))
+    prepare(X - 1)
+    for q in range(blocks):
+        last_halo(q).wait_recv()
+        complete(X - 1, q, False)
+        last_pair(q).start()
 
     level = levels_ref[0, 0]
     reach = 8
@@ -349,26 +438,35 @@
             return carry
         lax.fori_loop(0, B * blocks // 2, body, 0, unroll=2)
 
-    for n in range(zero + 1):
-        back_copy(n).wait_recv()
+    backs_done(0, X - H)
     for q in range(X // reach - 1):
         write(q * reach, reach)
-    reduce_pair(X - 1)
+    for q in range(blocks):
+        last_pair(q).wait_recv()
+        part[X - 1, kept(q)] = val[X - 1, own_rows(q)] + from_pair[X - 1, kept(q)]
+        for k in range(1, far):
+            last_far(q, k).start()
+    following.wait_recv()
+    shared.start()
+    finish_far(X - H, X - 1)
+    for q in range(blocks):
+        for k in range(1, far):
+            last_far(q, k).wait_recv()
+        summed = part[X - 1, kept(q)]
+        for k in range(1, far):
+            summed += from_far[k - 1, X - 1, kept(q)]
+        comb[X - 1, own_rows(q)] = summed
+        last_back(q).start()
     for side in range(2):
         whole = raw.at[pl.ds(0, H)]
-        remote(whole, whole, halo_send.at[side], halo_recv.at[side, 0], to(g, left)).wait_send()
-    finish_far(zero + 1, X - 1)
-    following.wait_recv()
-    shared.start()
-    reduce_far(X - 1)
-    for n in range(zero + 1, X - 1):
-        back_copy(n).wait_recv()
+        remote(whole, whole, halo_send.at[side], halo_recv.at[0], to(g, left)).wait_send()
+    backs_done(1, H - 1)
     shared.wait_recv()
     write(X - reach, reach - 1)
     following.wait_send()
+    shared.wait_send()
     remote(part, part, pair_send.at[0], pair_recv.at[0], to(pair, t)).wait_send()
-    shared.wait_send()
-    back_copy(X - 1).wait_recv()
+    backs_done(2, 1)
     for i in range(blocks):
         rows = pl.ds(i * B, B)
         o_ref[X - 1, rows] = jnp.where(level >= 4, comb[X - 1, rows], o_ref[X - 1, rows])
@@ -415,15 +513,16 @@
                 dma((2,)),
                 dma((LOADS,)),
                 dma((2,)),
-                dma((2, H)),
+                dma((2 * H + 4,)),
                 dma((1,)),
-                dma((X,)),
+                dma((8,)),
                 dma((far,)),
-                dma((far, X)),
+                dma((far, X + 3)),
                 dma((1,)),
-                dma((X,)),
+                dma((3,)),
                 dma((2,)),
                 dma((2,)),
+                pltpu.SemaphoreType.REGULAR,
                 pltpu.SemaphoreType.REGULAR,
             ],
             compiler_params=pltpu.CompilerParams(

time: 36.6 us -> 36 us (0.984)
  Pallas kernels: 34.5 us -> 33.9 us
    pallas_call x1, Pallas kernels: 34.5 us -> 33.9 us  [on_device(): pl.pallas_call(functools.partial(kernel, grids, tiles, X, B), out_shape=j...]
where the time goes in v3:
time: 36 us; the launch traced here: 35.9 us
  Pallas kernels  33.9 us (94%)
  local copies, waits for them, and re-layouts  1.32 us (4%)
  between operations  0.66 us (2%)
    pallas_call x1, Pallas kernels, on_device(): pl.pallas_call(functools.partial(kernel, grids, tiles, X, B), out_shape=j...  33.9 us
    unnamed x1, local copies, waits for them, and re-layouts  1.32 us

profile of v3, /device:TPU:0, one launch (start us, length us, event | category | flops | bytes accessed | tf_op | source)
XLA Modules:
  0.0 35.9 jit_solution(9032355783049128553)
XLA Ops:
  0.7 33.9 %shard_map.37 = f32[16,32,8,128]{3,2,1,0:T(8,128)S(1)} custom-call(s32[1,6]{1,0:T(1,128)} %levels_hbm.1, s32[1]{0:T(128)S(6)} %copy.5.sign_hbm, f32[16,32,8,128]{3,2,1,0:T(8,128)} %bitcast.3), custom_call_target="tpu_custom_call" | custom-call | tf_op jit(solution)/shard_map/pallas_call | solution.py:494
  34.5 1.3 %copy.6 = f32[1,16,4,4,4,4,128]{6,5,4,3,2,1,0:T(4,128)} copy(f32[1,16,4,4,4,4,128]{6,5,4,3,2,1,0:T(4,128)S(1)} %bitcast.2) | data formatting | bytes 4194304

commit v4 on v3

--- a/solution.py
+++ b/solution.py
@@ -25,7 +25,7 @@
     levels_hbm, sign_hbm, x_ref, o_ref,
     levels_ref, sign_ref, raw, pa, ma, pb, mb, rest, val, from_pair, part, from_far, comb,
     small_sem, load_sem, halo_send, halo_recv, pair_send, pair_recv, far_send, far_recv,
-    back_send, back_recv, next_send, next_recv, credit, met,
+    back_send, back_recv, next_recv, credit, met,
 ):
     H = STEPS
     g = lax.axis_index("grid")
@@ -83,17 +83,17 @@
         return remote(
             x_ref.at[(1 - side) * (X - 1 - k) + side * k],
             raw.at[(1 - side) * (H - 1 - k) + side * (X + H + k)],
-            halo_send.at[side], halo_recv.at[side * H + k],
+            halo_send.at[0], halo_recv.at[side * H + k],
             to(g, (t + 1 + side * (tiles - 2)) % tiles),
         )
 
     blocks = 4
 
-    def last_halo(q):
+    def last_halo(m, q):
         rows = pl.ds(q * B, B)
         return remote(
-            x_ref.at[H - 1, rows], raw.at[X + 2 * H - 1, rows],
-            halo_send.at[1], halo_recv.at[2 * H - 1 + q], to(g, left),
+            x_ref.at[H - 2 + m, rows], raw.at[X + 2 * H - 2 + m, rows],
+            halo_send.at[0], halo_recv.at[2 * H - 2 + blocks * m + q], to(g, left),
         )
 
     part_at = B
@@ -102,7 +102,7 @@
         rows = pl.ds(q * part_at, part_at - q * (2 * part_at - blocks * B))
         return remote(
             x_ref.at[X - 3, rows], raw.at[H - 3, rows],
-            halo_send.at[0], halo_recv.at[2 + q * (2 * H + 1)], to(g, right),
+            halo_send.at[0], halo_recv.at[2 + q * (2 * H + 4)], to(g, right),
         )
 
     def start_left():
@@ -114,10 +114,11 @@
             halo(0, k).start()
 
     def start_right():
-        for k in range(H - 1):
+        for k in range(H - 2):
             halo(1, k).start()
-        for q in range(blocks):
-            last_halo(q).start()
+        for m in range(2):
+            for q in range(blocks):
+                last_halo(m, q).start()
 
     sub = lax.broadcasted_iota(jnp.int32, (2, 8, 128), 1)
     low = sub < 4
@@ -240,7 +241,7 @@
         i = place(n)
         return remote(
             part.at[i], from_far.at[k - 1, i],
-            far_send.at[k - 1], far_recv.at[k - 1, n], to((g + 2 * k) % grids, t),
+            far_send.at[k - 1], far_recv.at[k - 1, jnp.minimum(n, X - H)], to((g + 2 * k) % grids, t),
         )
 
     def back_copy(n):
@@ -259,9 +260,10 @@
         for k in range(1, far):
             far_copy(n, k).start()
 
-    def reduce_far(n):
-        for k in range(1, far):
-            far_copy(n, k).wait_recv()
+    def reduce_far(n, waited=False):
+        if not waited:
+            for k in range(1, far):
+                far_copy(n, k).wait_recv()
         i = place(n)
         summed = part[i]
         for k in range(1, far):
@@ -280,21 +282,41 @@
     def kept(q):
         return pl.ds(q * small, small)
 
-    def last_pair(q):
-        return remote(
-            val.at[X - 1, other_rows(q)], from_pair.at[X - 1, kept(q)],
-            pair_send.at[0], pair_recv.at[4 + q], to(pair, t),
-        )
-
-    def last_far(q, k):
-        return remote(
-            part.at[X - 1, kept(q)], from_far.at[k - 1, X - 1, kept(q)],
-            far_send.at[k - 1], far_recv.at[k - 1, X - 1 + q], to((g + 2 * k) % grids, t),
-        )
-
-    def last_back(q):
-        own = comb.at[X - 1, own_rows(q)]
-        return remote(own, own, back_send.at[0], back_recv.at[2], to(pair, t))
+    def last_pair(m, q):
+        i = X - 2 + m
+        return remote(
+            val.at[i, other_rows(q)], from_pair.at[i, kept(q)],
+            pair_send.at[0], pair_recv.at[4 - 4 * m + q], to(pair, t),
+        )
+
+    def last_far(m, q, k):
+        i = X - 2 + m
+        return remote(
+            part.at[i, kept(q)], from_far.at[k - 1, i, kept(q)],
+            far_send.at[k - 1], far_recv.at[k - 1, X - H + m * (1 + q)], to((g + 2 * k) % grids, t),
+        )
+
+    def last_back(m, q):
+        own = comb.at[X - 2 + m, own_rows(q)]
+        return remote(own, own, back_send.at[0], back_recv.at[1 + m], to(pair, t))
+
+    def reduce_last_pair(m, q):
+        i = X - 2 + m
+        last_pair(m, q).wait_recv()
+        part[i, kept(q)] = val[i, own_rows(q)] + from_pair[i, kept(q)]
+        for k in range(1, far):
+            last_far(m, q, k).start()
+
+    def reduce_last_far(m, q):
+        i = X - 2 + m
+        if m == 1:
+            for k in range(1, far):
+                last_far(m, q, k).wait_recv()
+        summed = part[i, kept(q)]
+        for k in range(1, far):
+            summed += from_far[k - 1, i, kept(q)]
+        comb[i, own_rows(q)] = summed
+        last_back(m, q).start()
 
     ahead = [2, 2, 3, 5, 7, 9, 10]
     held = 5
@@ -312,8 +334,8 @@
             return carry
         lax.fori_loop(lo, hi, body, 0)
 
-    following = remote(comb.at[0, mine], comb.at[X, mine], next_send.at[0], next_recv.at[0], to(g, left))
-    shared = remote(comb.at[X, mine], comb.at[X, mine], next_send.at[1], next_recv.at[1], to(pair, t))
+    following = remote(comb.at[0, mine], comb.at[X, mine], back_send.at[0], next_recv.at[0], to(g, left))
+    shared = remote(comb.at[X, mine], comb.at[X, mine], back_send.at[0], next_recv.at[1], to(pair, t))
 
     for s in range(STEPS):
         def body(i, carry, s=s):
@@ -382,7 +404,6 @@
     def prepare(n):
         for s in range(STEPS):
             partly(s, n + 2 * H - 1 - s)
-        reduce_pair(n - 1)
 
     def complete(n, q, keep):
         rows = pl.ds(q * B, B)
@@ -400,6 +421,7 @@
     def ending(n, carry):
         j = n - inner
         prepare(n)
+        reduce_pair(n - 1)
         finish_far(done_before(j - 1), done_before(j))
         halo(1, n - (X - H)).wait_recv()
         for q in range(blocks):
@@ -407,14 +429,26 @@
         pair_copy(n).start()
         return carry
 
-    lax.fori_loop(X - H, X - 1, ending, 0)
+    lax.fori_loop(X - H, X - 2, ending, 0)
+    prepare(X - 2)
+    reduce_pair(X - 3)
+    finish_far(ahead[-2], ahead[-1])
+    for q in range(blocks):
+        last_halo(0, q).wait_recv()
+        complete(X - 2, q, True)
+        last_pair(0, q).start()
+        if q > 1:
+            reduce_last_pair(0, q - 2)
     finish_far(ahead[-1], X - H)
     following.start()
+    reduce_last_pair(0, blocks - 2)
     prepare(X - 1)
+    reduce_last_pair(0, blocks - 1)
     for q in range(blocks):
-        last_halo(q).wait_recv()
+        last_halo(1, q).wait_recv()
         complete(X - 1, q, False)
-        last_pair(q).start()
+        last_pair(1, q).start()
+    reduce_last_pair(1, 0)
 
     level = levels_ref[0, 0]
     reach = 8
@@ -441,30 +475,23 @@
     backs_done(0, X - H)
     for q in range(X // reach - 1):
         write(q * reach, reach)
-    for q in range(blocks):
-        last_pair(q).wait_recv()
-        part[X - 1, kept(q)] = val[X - 1, own_rows(q)] + from_pair[X - 1, kept(q)]
-        for k in range(1, far):
-            last_far(q, k).start()
+    for q in range(1, blocks):
+        reduce_last_pair(1, q)
     following.wait_recv()
     shared.start()
-    finish_far(X - H, X - 1)
-    for q in range(blocks):
-        for k in range(1, far):
-            last_far(q, k).wait_recv()
-        summed = part[X - 1, kept(q)]
-        for k in range(1, far):
-            summed += from_far[k - 1, X - 1, kept(q)]
-        comb[X - 1, own_rows(q)] = summed
-        last_back(q).start()
-    for side in range(2):
-        whole = raw.at[pl.ds(0, H)]
-        remote(whole, whole, halo_send.at[side], halo_recv.at[0], to(g, left)).wait_send()
+    some = part.at[pl.ds(0, H - 1)]
+    for k in range(1, far):
+        remote(some, some, far_send.at[k - 1], far_recv.at[k - 1, X - H], to(pair, t)).wait_recv()
+    for n in range(X - H, X - 2):
+        reduce_far(n, True)
+    for m in range(2):
+        for q in range(blocks):
+            reduce_last_far(m, q)
+    whole = raw.at[pl.ds(0, 2 * H)]
+    remote(whole, whole, halo_send.at[0], halo_recv.at[0], to(g, left)).wait_send()
     backs_done(1, H - 1)
     shared.wait_recv()
     write(X - reach, reach - 1)
-    following.wait_send()
-    shared.wait_send()
     remote(part, part, pair_send.at[0], pair_recv.at[0], to(pair, t)).wait_send()
     backs_done(2, 1)
     for i in range(blocks):
@@ -472,7 +499,8 @@
         o_ref[X - 1, rows] = jnp.where(level >= 4, comb[X - 1, rows], o_ref[X - 1, rows])
     for k in range(1, far):
         remote(part, part, far_send.at[k - 1], far_recv.at[k - 1, 0], to(pair, t)).wait_send()
-    remote(part, part, back_send.at[0], back_recv.at[0], to(pair, t)).wait_send()
+    whole = raw.at[pl.ds(0, X // 2 + 1)]
+    remote(whole, whole, back_send.at[0], back_recv.at[0], to(pair, t)).wait_send()
 
 
 def solution(mesh):
@@ -512,15 +540,14 @@
                 pltpu.VMEM((X + 1, *field), f32),
                 dma((2,)),
                 dma((LOADS,)),
-                dma((2,)),
-                dma((2 * H + 4,)),
+                dma((1,)),
+                dma((2 * H + 7,)),
                 dma((1,)),
                 dma((8,)),
                 dma((far,)),
-                dma((far, X + 3)),
+                dma((far, X - H + 5)),
                 dma((1,)),
                 dma((3,)),
-                dma((2,)),
                 dma((2,)),
                 pltpu.SemaphoreType.REGULAR,
                 pltpu.SemaphoreType.REGULAR,

time: 36 us -> 35.4 us (0.983)
  Pallas kernels: 33.9 us -> 33.3 us
    pallas_call x1, Pallas kernels: 33.9 us -> 33.3 us  [on_device(): pl.pallas_call(functools.partial(kernel, grids, tiles, X, B), out_shape=j...]
where the time goes in v4:
time: 35.4 us; the launch traced here: 35.3 us
  Pallas kernels  33.3 us (94%)
  local copies, waits for them, and re-layouts  1.32 us (4%)
  between operations  0.66 us (2%)
    pallas_call x1, Pallas kernels, on_device(): pl.pallas_call(functools.partial(kernel, grids, tiles, X, B), out_shape=j...  33.3 us
    unnamed x1, local copies, waits for them, and re-layouts  1.32 us

profile of v4, /device:TPU:0, one launch (start us, length us, event | category | flops | bytes accessed | tf_op | source)
XLA Modules:
  0.0 35.3 jit_solution(2327645132697082838)
XLA Ops:
  0.7 33.3 %shard_map.37 = f32[16,32,8,128]{3,2,1,0:T(8,128)S(1)} custom-call(s32[1,6]{1,0:T(1,128)} %levels_hbm.1, s32[1]{0:T(128)S(6)} %copy.5.sign_hbm, f32[16,32,8,128]{3,2,1,0:T(8,128)} %bitcast.3), custom_call_target="tpu_custom_call" | custom-call | tf_op jit(solution)/shard_map/pallas_call | solution.py:522
  33.9 1.3 %copy.6 = f32[1,16,4,4,4,4,128]{6,5,4,3,2,1,0:T(4,128)} copy(f32[1,16,4,4,4,4,128]{6,5,4,3,2,1,0:T(4,128)S(1)} %bitcast.2) | data formatting | bytes 4194304

commit v5 on v4

--- a/solution.py
+++ b/solution.py
@@ -22,7 +22,7 @@
 
 def kernel(
     grids, tiles, X, B,
-    levels_hbm, sign_hbm, x_ref, o_ref,
+    levels_hbm, sign_hbm, x_ref, o_ref, stage_ref,
     levels_ref, sign_ref, raw, pa, ma, pb, mb, rest, val, from_pair, part, from_far, comb,
     small_sem, load_sem, halo_send, halo_recv, pair_send, pair_recv, far_send, far_recv,
     back_send, back_recv, next_recv, credit, met,
@@ -122,8 +122,13 @@
 
     sub = lax.broadcasted_iota(jnp.int32, (2, 8, 128), 1)
     low = sub < 4
-    first = sub % 4 == 0
-    last = sub % 4 == 3
+    place_in = lax.broadcasted_iota(jnp.int32, (8, 128), 0)
+    up = place_in // 4 * 4 + (place_in + 1) % 4
+    down = place_in // 4 * 4 + (place_in + 3) % 4
+
+    def turned(v, where):
+        return jnp.stack([jnp.take_along_axis(v[i], where, axis=0) for i in range(2)])
+
     fine = blocks * blocks
 
     def split(v, p_ref, m_ref, layer, rows):
@@ -195,12 +200,9 @@
             p_ref[layer, at_rows(i1 + (i2 + 1) % blocks)]
             + m_ref[layer, at_rows(i1 + (i2 + blocks - 1) % blocks)]
         )
-        ph = pltpu.roll(p, 4, 1)
-        mh = pltpu.roll(m, 4, 1)
-        acc += rates[3] * (jnp.where(low, ph, swapped(ph)) + jnp.where(low, swapped(mh), mh))
-        p4 = pltpu.roll(jnp.where(first, ph, p), 7, 1)
-        m4 = pltpu.roll(jnp.where(last, mh, m), 1, 1)
-        acc += rates[4] * (p4 + m4)
+        crossed = jnp.where(low, swapped(p), p) + jnp.where(low, m, swapped(m))
+        acc += rates[3] * pltpu.roll(crossed, 4, 1)
+        acc += rates[4] * (turned(p, up) + turned(m, down))
         acc += rates[5] * (p5 + m5)
         return acc, rows
 
@@ -334,7 +336,8 @@
             return carry
         lax.fori_loop(lo, hi, body, 0)
 
-    following = remote(comb.at[0, mine], comb.at[X, mine], back_send.at[0], next_recv.at[0], to(g, left))
+    staged = pltpu.make_async_copy(comb.at[0, mine], stage_ref, small_sem.at[0])
+    following = remote(stage_ref, comb.at[X, mine], back_send.at[0], next_recv.at[0], to(g, left))
     shared = remote(comb.at[X, mine], comb.at[X, mine], back_send.at[0], next_recv.at[1], to(pair, t))
 
     for s in range(STEPS):
@@ -389,6 +392,10 @@
         convert(at + H)
         for s in range(STEPS):
             step(s, at - back * (s + 1) + H)
+            if s == 1:
+                @pl.when((n == 1) & (core == 0))
+                def _():
+                    reduce_pair(0)
         pair_copy(n).start()
 
         @pl.when((odd == 0) & (t > 0) & (j == 1))
@@ -396,7 +403,9 @@
             pl.semaphore_wait(credit, 1)
             start_right()
 
-        reduce_pair(n - 1)
+        @pl.when((n > 1) | (core == 1))
+        def _():
+            reduce_pair(n - 1)
         return carry
 
     lax.fori_loop(1, X - H, wave, 0)
@@ -440,9 +449,11 @@
         if q > 1:
             reduce_last_pair(0, q - 2)
     finish_far(ahead[-1], X - H)
-    following.start()
+    staged.start()
     reduce_last_pair(0, blocks - 2)
     prepare(X - 1)
+    staged.wait()
+    following.start()
     reduce_last_pair(0, blocks - 1)
     for q in range(blocks):
         last_halo(1, q).wait_recv()
@@ -519,11 +530,11 @@
         dma = pltpu.SemaphoreType.DMA
         state = pltpu.with_memory_space_constraint(state_field.reshape(X, *field), pltpu.HBM)
         levels = pltpu.with_memory_space_constraint(levels, pltpu.HBM)
-        result = pl.pallas_call(
+        result, _ = pl.pallas_call(
             functools.partial(kernel, grids, tiles, X, B),
-            out_shape=jax.ShapeDtypeStruct((X, *field), f32),
+            out_shape=[jax.ShapeDtypeStruct((X, *field), f32), pltpu.HBM(halved, f32)],
             in_specs=[pl.BlockSpec(memory_space=pltpu.HBM)] * 3,
-            out_specs=pl.BlockSpec(memory_space=pltpu.VMEM),
+            out_specs=[pl.BlockSpec(memory_space=pltpu.VMEM), pl.BlockSpec(memory_space=pltpu.HBM)],
             scratch_shapes=[
                 pltpu.SMEM(levels.shape, jnp.int32),
                 pltpu.SMEM(sign_bits.shape, jnp.int32),

time: 35.4 us -> 35.4 us (level)
  no operation moved by 1% of the time
where the time goes in v5:
time: 35.4 us; the launch traced here: 35.3 us
  Pallas kernels  33.3 us (94%)
  local copies, waits for them, and re-layouts  1.32 us (4%)
  between operations  0.66 us (2%)
    pallas_call x1, Pallas kernels, on_device(): pl.pallas_call(functools.partial(kernel, grids, tiles, X, B), out_shape=[...  33.3 us
    unnamed x1, local copies, waits for them, and re-layouts  1.32 us

profile of v5, /device:TPU:0, one launch (start us, length us, event | category | flops | bytes accessed | tf_op | source)
XLA Modules:
  0.0 35.3 jit_solution(2786729478695416940)
XLA Ops:
  0.7 33.3 %shard_map.37 = (f32[16,32,8,128]{3,2,1,0:T(8,128)S(1)}, f32[16,8,128]{2,1,0:T(8,128)}) custom-call(s32[1,6]{1,0:T(1,128)} %levels_hbm.1, s32[1]{0:T(128)S(6)} %copy.5.sign_hbm, f32[16,32,8,128]{3,2,1,0:T(8,128)} %bitcast.3), custom_call_target="tpu_custom_call" | custom-call | tf_op jit(solution)/shard_map/pallas_call | solution.py:533
  33.9 1.3 %copy.6 = f32[1,16,4,4,4,4,128]{6,5,4,3,2,1,0:T(4,128)} copy(f32[1,16,4,4,4,4,128]{6,5,4,3,2,1,0:T(4,128)S(1)} %bitcast.2) | data formatting | bytes 4194304

commit v6 on v5

--- a/solution.py
+++ b/solution.py
@@ -22,8 +22,8 @@
 
 def kernel(
     grids, tiles, X, B,
-    levels_hbm, sign_hbm, x_ref, o_ref, stage_ref,
-    levels_ref, sign_ref, raw, pa, ma, pb, mb, rest, val, from_pair, part, from_far, comb,
+    levels_hbm, sign_ref, x_ref, o_ref, stage_ref,
+    levels_ref, raw, pa, ma, pb, mb, rest, val, from_pair, part, from_far, comb,
     small_sem, load_sem, halo_send, halo_recv, pair_send, pair_recv, far_send, far_recv,
     back_send, back_recv, next_recv, credit, met,
 ):
@@ -53,10 +53,8 @@
         )
 
     load_levels = pltpu.make_async_copy(levels_hbm, levels_ref, small_sem.at[0])
-    load_sign = pltpu.make_async_copy(sign_hbm, sign_ref, small_sem.at[1])
     load(0).start()
     load_levels.start()
-    load_sign.start()
     barrier = pltpu.get_barrier_semaphore()
 
     def greet(other):
@@ -167,7 +165,6 @@
         load(lo // piece).wait()
         convert_from(lo, min(lo + piece, 2 * H + 1))
     load_levels.wait()
-    load_sign.wait()
 
     rates = [ALPHA * rate_of(levels_ref[0, d]) for d in range(6)]
     total = rates[0] + rates[1] + rates[2] + rates[3] + rates[4] + rates[5]
@@ -533,11 +530,10 @@
         result, _ = pl.pallas_call(
             functools.partial(kernel, grids, tiles, X, B),
             out_shape=[jax.ShapeDtypeStruct((X, *field), f32), pltpu.HBM(halved, f32)],
-            in_specs=[pl.BlockSpec(memory_space=pltpu.HBM)] * 3,
+            in_specs=[pl.BlockSpec(memory_space=m) for m in (pltpu.HBM, pltpu.SMEM, pltpu.HBM)],
             out_specs=[pl.BlockSpec(memory_space=pltpu.VMEM), pl.BlockSpec(memory_space=pltpu.HBM)],
             scratch_shapes=[
                 pltpu.SMEM(levels.shape, jnp.int32),
-                pltpu.SMEM(sign_bits.shape, jnp.int32),
                 pltpu.VMEM((X + 2 * H, *field), f32),
                 pltpu.VMEM((X + 2 * H, *field), f32),
                 pltpu.VMEM((X + 2 * H, *field), f32),
@@ -549,7 +545,7 @@
                 pltpu.VMEM((X, *halved), f32),
                 pltpu.VMEM((far, X, *halved), f32),
                 pltpu.VMEM((X + 1, *field), f32),
-                dma((2,)),
+                dma((1,)),
                 dma((LOADS,)),
                 dma((1,)),
                 dma((2 * H + 7,)),

time: 35.4 us -> 35.4 us (level)
  no operation moved by 1% of the time
where the time goes in v6:
time: 35.4 us; the launch traced here: 35.2 us
  Pallas kernels  33.3 us (94%)
  local copies, waits for them, and re-layouts  1.32 us (4%)
  between operations  0.66 us (2%)
    pallas_call x1, Pallas kernels, on_device(): pl.pallas_call(functools.partial(kernel, grids, tiles, X, B), out_shape=[...  33.3 us
    unnamed x1, local copies, waits for them, and re-layouts  1.32 us

profile of v6, /device:TPU:0, one launch (start us, length us, event | category | flops | bytes accessed | tf_op | source)
XLA Modules:
  0.0 35.2 jit_solution(5649831991355961447)
XLA Ops:
  0.7 33.3 %shard_map.37 = (f32[16,32,8,128]{3,2,1,0:T(8,128)S(1)}, f32[16,8,128]{2,1,0:T(8,128)}) custom-call(s32[1,6]{1,0:T(1,128)} %levels_hbm.1, s32[1]{0:T(128)S(6)} %copy.5.sign_ref, f32[16,32,8,128]{3,2,1,0:T(8,128)} %bitcast.3), custom_call_target="tpu_custom_call" | custom-call | tf_op jit(solution)/shard_map/pallas_call | solution.py:530
  33.9 1.3 %copy.6 = f32[1,16,4,4,4,4,128]{6,5,4,3,2,1,0:T(4,128)} copy(f32[1,16,4,4,4,4,128]{6,5,4,3,2,1,0:T(4,128)S(1)} %bitcast.2) | data formatting | bytes 4194304
